TPU v7x, 32 devices: a whole 2x2x4 slice. The times are simulated.
32 devices in a mesh: dp: 8 (over y, x, core), fsdp: 4 (over z).
Axes of the slice: x: 2, y: 2, z: 4, core: 2. Of those that a mesh axis runs over, the one named last changes fastest.
Arguments:
- patches: bfloat16 [2, 2048, 1152], P(None, ('dp', 'fsdp')), may hold values from -6 to 6
- cotangent: bfloat16 [2, 2048, 1152], P(None, ('dp', 'fsdp')), may hold values from -6 to 6
- conditioning: float32 [2, 8, 1152], replicated, may hold values from -6 to 6
- frame_of_slot: int32 [2, 2048], P(None, ('dp', 'fsdp')), may hold values from 0 to 127, as said below
- clip_of_slot: int32 [2, 2048], P(None, ('dp', 'fsdp')), may hold values from 0 to 7, as said below
- w_ada: bfloat16 [1152, 6912], P('dp', 'fsdp'), may hold values from -0.1875 to 0.1875
- b_ada: bfloat16 [6912], P('fsdp'), may hold values from -3 to 3
- w_qkv: bfloat16 [1152, 3456], P('dp', 'fsdp'), may hold values from -0.1875 to 0.1875
- b_qv: bfloat16 [2304], P('fsdp'), may hold values from -2 to 2
- w_proj: bfloat16 [1152, 1152], P('dp', 'fsdp'), may hold values from -1 to 1
- b_proj: bfloat16 [1152], P('fsdp'), may hold values from -2 to 2
- w_fc1: bfloat16 [1152, 4608], P('dp', 'fsdp'), may hold values from -0.1875 to 0.1875
- b_fc1: bfloat16 [4608], P('fsdp'), may hold values from -3 to 3
- w_fc2: bfloat16 [4608, 1152], P('dp', 'fsdp'), may hold values from -0.09375 to 0.09375
- b_fc2: bfloat16 [1152], P('fsdp'), may hold values from -2 to 2
Outputs:
- output: bfloat16 [2, 2048, 1152], P(None, ('dp', 'fsdp'))
- input_grad: bfloat16 [2, 2048, 1152], P(None, ('dp', 'fsdp'))
- cond_grad: float32 [2, 8, 1152], P(None, None, 'fsdp')
- grad_w_ada: float32 [1152, 6912], P('dp', 'fsdp')
- grad_b_ada: float32 [6912], P('fsdp')
- grad_w_qkv: float32 [1152, 3456], P('dp', 'fsdp')
- grad_b_qv: float32 [2304], P('fsdp')
- grad_w_proj: float32 [1152, 1152], P('dp', 'fsdp')
- grad_b_proj: float32 [1152], P('fsdp')
- grad_w_fc1: float32 [1152, 4608], P('dp', 'fsdp')
- grad_b_fc1: float32 [4608], P('fsdp')
- grad_w_fc2: float32 [4608, 1152], P('dp', 'fsdp')
- grad_b_fc2: float32 [1152], P('fsdp')
Inputs may be any that keep to these rules, and one draw needn't show every extreme that they name: `frame_of_slot`: in each micro-batch, each aligned block of 64 slots holds either one frame of 64 patches or four frames of 16 patches one after another; no frame number appears in two blocks. `clip_of_slot`: all slots of one frame name the same clip.
All inputs are finite; a program needn't handle non-finite values.
Results may differ from a plain program's by a relative error of at most 0.018.
Values may be sent and summed in bfloat16 or wider, within the bound.
A program may use at most 256 MiB of HBM per device.

v0:
```python
import math
import jax
import jax.numpy as jnp
from jax import lax
from jax.sharding import PartitionSpec as P

HEAD_DIM = 72
EPS = 1e-06
GELU_C = math.sqrt(2.0 / math.pi)
PRECISE = lax.Precision.HIGHEST
NEG_FILL = -1e30


def layer_norm(values):
    centre = values - jnp.mean(values, axis=-1, keepdims=True)
    return centre * lax.rsqrt(jnp.mean(centre * centre, axis=-1, keepdims=True) + EPS)


def gelu_tanh(hidden):
    return 0.5 * hidden * (1.0 + jnp.tanh(GELU_C * (hidden + 0.044715 * hidden * hidden * hidden)))


def modulate(values, shift_part, scale_part):
    return layer_norm(values) * (1.0 + scale_part) + shift_part


def matmul_plain(left, right):
    return jnp.dot(left, right, preferred_element_type=jnp.float32)


def matmul_right_t(left, right):
    return lax.dot_general(
        left, right, (((1,), (1,)), ((), ())), preferred_element_type=jnp.float32
    )


def matmul_left_t(left, right):
    return lax.dot_general(
        left, right, (((0,), (0,)), ((), ())), preferred_element_type=jnp.float32
    )


def precise_left_t(left, right):
    return lax.dot_general(
        left, right, (((0,), (0,)), ((), ())), precision=PRECISE, preferred_element_type=jnp.float32
    )


def precise_right_t(left, right):
    return lax.dot_general(
        left, right, (((1,), (1,)), ((), ())), precision=PRECISE, preferred_element_type=jnp.float32
    )


def gather_weights(w_qkv, w_proj, w_fc1, w_fc2, b_qv, b_proj, b_fc1, b_fc2):
    inner_parts = (
        lax.all_gather(w_qkv, "fsdp", axis=1, tiled=True),
        lax.all_gather(w_proj, "fsdp", axis=1, tiled=True),
        lax.all_gather(w_fc1, "fsdp", axis=1, tiled=True),
        lax.all_gather(w_fc2, "fsdp", axis=1, tiled=True),
        lax.all_gather(b_qv, "fsdp", axis=0, tiled=True),
        lax.all_gather(b_proj, "fsdp", axis=0, tiled=True),
        lax.all_gather(b_fc1, "fsdp", axis=0, tiled=True),
        lax.all_gather(b_fc2, "fsdp", axis=0, tiled=True),
    )
    whole_rows = (
        lax.all_gather(inner_parts[0], "dp", axis=0, tiled=True),
        lax.all_gather(inner_parts[1], "dp", axis=0, tiled=True),
        lax.all_gather(inner_parts[2], "dp", axis=0, tiled=True),
        lax.all_gather(inner_parts[3], "dp", axis=0, tiled=True),
    )
    return (
        whole_rows[0],
        whole_rows[1],
        whole_rows[2],
        whole_rows[3],
        inner_parts[4],
        inner_parts[5],
        inner_parts[6],
        inner_parts[7],
    )


def reduce_grads(full_w, full_b):
    inner_sums = (
        lax.psum_scatter(
            full_w[0].astype(jnp.bfloat16), "fsdp", scatter_dimension=1, tiled=True
        ).astype(jnp.float32),
        lax.psum_scatter(
            full_w[1].astype(jnp.bfloat16), "fsdp", scatter_dimension=1, tiled=True
        ).astype(jnp.float32),
        lax.psum_scatter(
            full_w[2].astype(jnp.bfloat16), "fsdp", scatter_dimension=1, tiled=True
        ).astype(jnp.float32),
        lax.psum_scatter(
            full_w[3].astype(jnp.bfloat16), "fsdp", scatter_dimension=1, tiled=True
        ).astype(jnp.float32),
        lax.psum_scatter(
            full_b[0].astype(jnp.bfloat16), "fsdp", scatter_dimension=0, tiled=True
        ).astype(jnp.float32),
        lax.psum_scatter(
            full_b[1].astype(jnp.bfloat16), "fsdp", scatter_dimension=0, tiled=True
        ).astype(jnp.float32),
        lax.psum_scatter(
            full_b[2].astype(jnp.bfloat16), "fsdp", scatter_dimension=0, tiled=True
        ).astype(jnp.float32),
        lax.psum_scatter(
            full_b[3].astype(jnp.bfloat16), "fsdp", scatter_dimension=0, tiled=True
        ).astype(jnp.float32),
    )
    outer_sums = (
        lax.psum_scatter(
            inner_sums[0].astype(jnp.bfloat16), "dp", scatter_dimension=0, tiled=True
        ).astype(jnp.float32),
        lax.psum_scatter(
            inner_sums[1].astype(jnp.bfloat16), "dp", scatter_dimension=0, tiled=True
        ).astype(jnp.float32),
        lax.psum_scatter(
            inner_sums[2].astype(jnp.bfloat16), "dp", scatter_dimension=0, tiled=True
        ).astype(jnp.float32),
        lax.psum_scatter(
            inner_sums[3].astype(jnp.bfloat16), "dp", scatter_dimension=0, tiled=True
        ).astype(jnp.float32),
    )
    small_sums = lax.psum((inner_sums[4], inner_sums[5], inner_sums[6], inner_sums[7]), "dp")
    return (tuple(outer_sums), tuple(small_sums))


def modulation_sharded(silu_low, w_ada, b_ada):
    row_width, col_width = w_ada.shape
    row_start = lax.axis_index("dp") * row_width
    col_start = lax.axis_index("fsdp") * col_width
    silu_part = lax.dynamic_slice_in_dim(silu_low, row_start, row_width, 1)
    partial_value = matmul_plain(silu_part, w_ada)
    bias_term = jnp.where(
        lax.axis_index("dp") == 0, b_ada.astype(jnp.float32), jnp.zeros((col_width,), jnp.float32)
    )
    partial_value = partial_value + bias_term[None, :]
    padded = jnp.zeros((silu_low.shape[0], col_width * lax.axis_size("fsdp")), jnp.float32)
    padded = lax.dynamic_update_slice_in_dim(padded, partial_value, col_start, 1)
    return lax.psum(padded, ("dp", "fsdp"))


def ada_grads_sharded(silu_low, cond_rows, d_modulation, w_ada):
    row_width, col_width = w_ada.shape
    row_start = lax.axis_index("dp") * row_width
    col_start = lax.axis_index("fsdp") * col_width
    d_total = lax.psum(d_modulation, ("dp", "fsdp"))
    d_cols = lax.dynamic_slice_in_dim(d_total, col_start, col_width, 1)
    silu_part = lax.dynamic_slice_in_dim(silu_low, row_start, row_width, 1).astype(jnp.float32)
    grad_weight = precise_left_t(silu_part, d_cols)
    grad_bias = jnp.sum(d_cols, axis=0)
    d_silu_part = precise_right_t(d_cols, w_ada.astype(jnp.float32))
    model_width = cond_rows.shape[1]
    padded = jnp.zeros((cond_rows.shape[0], model_width), jnp.float32)
    padded = lax.dynamic_update_slice_in_dim(padded, d_silu_part, row_start, 1)
    d_silu = lax.psum(padded, ("dp", "fsdp"))
    own_width = model_width // lax.axis_size("fsdp")
    own_start = lax.axis_index("fsdp") * own_width
    d_silu_own = lax.dynamic_slice_in_dim(d_silu, own_start, own_width, 1)
    cond_own = lax.dynamic_slice_in_dim(cond_rows, own_start, own_width, 1)
    silu_own, silu_own_back = jax.vjp(jax.nn.silu, cond_own)
    cond_grad = silu_own_back(d_silu_own)[0]
    return (grad_weight, grad_bias, cond_grad)


def head_scores(queries, key_rows, same_frame):
    scores = jnp.einsum(
        "qhd,khd->hqk", queries, key_rows, preferred_element_type=jnp.float32
    ) * HEAD_DIM ** (-0.5)
    return jnp.where(same_frame[None, :, :], scores, NEG_FILL)


def micro_forward(patch_rows, modulation, frame_ids, clip_ids, weights):
    w_qkv, w_proj, w_fc1, w_fc2, b_qv, b_proj, b_fc1, b_fc2 = weights
    row_count, model_width = patch_rows.shape
    head_count = model_width // HEAD_DIM
    clip_hot = (
        clip_ids[:, None] == jnp.arange(modulation.shape[0], dtype=jnp.int32)[None, :]
    ).astype(jnp.float32)
    token_mod = jnp.dot(clip_hot, modulation, precision=PRECISE)
    shift_one, scale_one, gate_one, shift_two, scale_two, gate_two = jnp.split(token_mod, 6, axis=1)
    inputs_float = patch_rows.astype(jnp.float32)
    attn_in, norm_one_back = jax.vjp(modulate, inputs_float, shift_one, scale_one)
    attn_low = attn_in.astype(jnp.bfloat16)
    qkv_bias = jnp.concatenate(
        [b_qv[:model_width], jnp.zeros((model_width,), jnp.bfloat16), b_qv[model_width:]]
    ).astype(jnp.float32)
    qkv_low = (matmul_plain(attn_low, w_qkv) + qkv_bias).astype(jnp.bfloat16)
    queries = qkv_low[:, :model_width].reshape(row_count, head_count, HEAD_DIM)
    key_rows = qkv_low[:, model_width : 2 * model_width].reshape(row_count, head_count, HEAD_DIM)
    value_rows = qkv_low[:, 2 * model_width :].reshape(row_count, head_count, HEAD_DIM)
    same_frame = frame_ids[:, None] == frame_ids[None, :]
    scores = head_scores(queries, key_rows, same_frame)
    row_max = jnp.max(scores, axis=-1, keepdims=True)
    exp_scores = jnp.exp(scores - row_max)
    exp_total = jnp.sum(exp_scores, axis=-1, keepdims=True)
    shares = exp_scores / exp_total
    log_total = row_max + jnp.log(exp_total)
    mixed_low = (
        jnp.einsum(
            "hqk,khd->qhd",
            shares.astype(jnp.bfloat16),
            value_rows,
            preferred_element_type=jnp.float32,
        )
        .reshape(row_count, model_width)
        .astype(jnp.bfloat16)
    )
    attn_out = matmul_plain(mixed_low, w_proj) + b_proj.astype(jnp.float32)
    after_attn = inputs_float + gate_one * attn_out
    mlp_in, norm_two_back = jax.vjp(modulate, after_attn, shift_two, scale_two)
    mlp_low = mlp_in.astype(jnp.bfloat16)
    hidden = matmul_plain(mlp_low, w_fc1) + b_fc1.astype(jnp.float32)
    act_value, gelu_back = jax.vjp(gelu_tanh, hidden)
    act_low = act_value.astype(jnp.bfloat16)
    branch = matmul_plain(act_low, w_fc2) + b_fc2.astype(jnp.float32)
    output = (after_attn + gate_two * branch).astype(jnp.bfloat16)
    saved = (
        clip_hot,
        gate_one,
        gate_two,
        norm_one_back,
        attn_low,
        queries,
        key_rows,
        value_rows,
        same_frame,
        log_total,
        mixed_low,
        attn_out,
        norm_two_back,
        mlp_low,
        gelu_back,
        act_low,
        branch,
    )
    return (output, saved)


def micro_backward(saved, cot_rows, weights):
    w_qkv, w_proj, w_fc1, w_fc2 = (weights[0], weights[1], weights[2], weights[3])
    (
        clip_hot,
        gate_one,
        gate_two,
        norm_one_back,
        attn_low,
        queries,
        key_rows,
        value_rows,
        same_frame,
        log_total,
        mixed_low,
        attn_out,
        norm_two_back,
        mlp_low,
        gelu_back,
        act_low,
        branch,
    ) = saved
    row_count = cot_rows.shape[0]
    model_width = cot_rows.shape[1]
    head_count = model_width // HEAD_DIM
    cot_float = cot_rows.astype(jnp.float32)
    d_branch = (gate_two * cot_float).astype(jnp.bfloat16)
    grad_gate_two = cot_float * branch
    grad_w_fc2 = matmul_left_t(act_low, d_branch)
    grad_b_fc2 = jnp.sum(d_branch.astype(jnp.float32), axis=0)
    d_act = matmul_right_t(d_branch, w_fc2)
    d_hidden = gelu_back(d_act)[0].astype(jnp.bfloat16)
    grad_w_fc1 = matmul_left_t(mlp_low, d_hidden)
    grad_b_fc1 = jnp.sum(d_hidden.astype(jnp.float32), axis=0)
    d_mlp = matmul_right_t(d_hidden, w_fc1)
    d_after, d_shift_two, d_scale_two = norm_two_back(d_mlp)
    d_after = cot_float + d_after
    grad_gate_one = d_after * attn_out
    d_attn = (gate_one * d_after).astype(jnp.bfloat16)
    grad_w_proj = matmul_left_t(mixed_low, d_attn)
    grad_b_proj = jnp.sum(d_attn.astype(jnp.float32), axis=0)
    d_mix = (
        matmul_right_t(d_attn, w_proj).astype(jnp.bfloat16).reshape(row_count, head_count, HEAD_DIM)
    )
    shares_again = jnp.exp(head_scores(queries, key_rows, same_frame) - log_total)
    d_shares = jnp.einsum("qhd,khd->hqk", d_mix, value_rows, preferred_element_type=jnp.float32)
    row_delta = jnp.sum(shares_again * d_shares, axis=-1, keepdims=True)
    d_scores = (shares_again * (d_shares - row_delta)).astype(jnp.bfloat16)
    d_queries = jnp.einsum(
        "hqk,khd->qhd", d_scores, key_rows, preferred_element_type=jnp.float32
    ) * HEAD_DIM ** (-0.5)
    d_keys = jnp.einsum(
        "hqk,qhd->khd", d_scores, queries, preferred_element_type=jnp.float32
    ) * HEAD_DIM ** (-0.5)
    d_values = jnp.einsum(
        "hqk,qhd->khd", shares_again.astype(jnp.bfloat16), d_mix, preferred_element_type=jnp.float32
    )
    d_qkv = jnp.concatenate(
        [
            d_queries.reshape(row_count, model_width),
            d_keys.reshape(row_count, model_width),
            d_values.reshape(row_count, model_width),
        ],
        axis=1,
    ).astype(jnp.bfloat16)
    grad_w_qkv = matmul_left_t(attn_low, d_qkv)
    column_sums = jnp.sum(d_qkv.astype(jnp.float32), axis=0)
    grad_b_qv = jnp.concatenate([column_sums[:model_width], column_sums[2 * model_width :]])
    d_attn_in = matmul_right_t(d_qkv, w_qkv)
    d_inputs, d_shift_one, d_scale_one = norm_one_back(d_attn_in)
    input_grad = (d_after + d_inputs).astype(jnp.bfloat16)
    d_token_mod = jnp.concatenate(
        [d_shift_one, d_scale_one, grad_gate_one, d_shift_two, d_scale_two, grad_gate_two], axis=1
    )
    d_modulation = lax.dot_general(
        clip_hot,
        d_token_mod,
        (((0,), (0,)), ((), ())),
        precision=PRECISE,
        preferred_element_type=jnp.float32,
    )
    grads_w = (grad_w_qkv, grad_w_proj, grad_w_fc1, grad_w_fc2)
    grads_b = (grad_b_qv, grad_b_proj, grad_b_fc1, grad_b_fc2)
    return (input_grad, d_modulation, grads_w, grads_b)


def add_terms(first_terms, second_terms):
    if first_terms is None:
        return tuple(second_terms)
    return tuple(
        (first_item + second_item for first_item, second_item in zip(first_terms, second_terms))
    )


def per_device(
    patches,
    cotangent,
    conditioning,
    frame_of_slot,
    clip_of_slot,
    w_ada,
    b_ada,
    w_qkv,
    b_qv,
    w_proj,
    b_proj,
    w_fc1,
    b_fc1,
    w_fc2,
    b_fc2,
):
    micro_count = patches.shape[0]
    outputs = []
    input_grads = []
    cond_parts = []
    summed_w = None
    summed_b = None
    ada_terms = None
    for micro_index in range(micro_count):
        cond_rows = conditioning[micro_index]
        silu_value, silu_back = jax.vjp(jax.nn.silu, cond_rows)
        silu_low = silu_value.astype(jnp.bfloat16)
        weights = gather_weights(w_qkv, w_proj, w_fc1, w_fc2, b_qv, b_proj, b_fc1, b_fc2)
        modulation = modulation_sharded(silu_low, w_ada, b_ada)
        output, saved = micro_forward(
            patches[micro_index],
            modulation,
            frame_of_slot[micro_index],
            clip_of_slot[micro_index],
            weights,
        )
        input_grad, d_modulation, grads_w, grads_b = micro_backward(
            saved, cotangent[micro_index], weights
        )
        outputs.append(output)
        input_grads.append(input_grad)
        grad_w_ada, grad_b_ada, cond_grad = ada_grads_sharded(
            silu_low, cond_rows, d_modulation, w_ada
        )
        cond_parts.append(cond_grad[None])
        ada_terms = add_terms(ada_terms, (grad_w_ada, grad_b_ada))
        part_w, part_b = reduce_grads(grads_w, grads_b)
        summed_w = add_terms(summed_w, part_w)
        summed_b = add_terms(summed_b, part_b)
    cond_all = jnp.concatenate(cond_parts, axis=0)
    return (
        jnp.stack(outputs),
        jnp.stack(input_grads),
        cond_all,
        ada_terms[0],
        ada_terms[1],
        summed_w[0],
        summed_b[0],
        summed_w[1],
        summed_b[1],
        summed_w[2],
        summed_b[2],
        summed_w[3],
        summed_b[3],
    )


def solution(mesh):
    in_specs = (
        P(None, ("dp", "fsdp"), None),
        P(None, ("dp", "fsdp"), None),
        P(),
        P(None, ("dp", "fsdp")),
        P(None, ("dp", "fsdp")),
        P("dp", "fsdp"),
        P("fsdp"),
        P("dp", "fsdp"),
        P("fsdp"),
        P("dp", "fsdp"),
        P("fsdp"),
        P("dp", "fsdp"),
        P("fsdp"),
        P("dp", "fsdp"),
        P("fsdp"),
    )
    out_specs = (
        P(None, ("dp", "fsdp"), None),
        P(None, ("dp", "fsdp"), None),
        P(None, None, "fsdp"),
        P("dp", "fsdp"),
        P("fsdp"),
        P("dp", "fsdp"),
        P("fsdp"),
        P("dp", "fsdp"),
        P("fsdp"),
        P("dp", "fsdp"),
        P("fsdp"),
        P("dp", "fsdp"),
        P("fsdp"),
    )
    return jax.shard_map(
        per_device, mesh=mesh, in_specs=in_specs, out_specs=out_specs, check_vma=False
    )
```

profile of v0, /device:TPU:0, one launch (start us, length us, event | category | flops | bytes accessed | tf_op | source)
XLA Modules:
  0.0 1921.0 jit_solution(4469489425580298956)
XLA Ops:
  14.6 38.8 %all-gather = bf16[4,864,144]{1,2,0:T(8,128)(2,1)S(1)} all-gather(bf16[1,864,144]{1,2,0:T(8,128)(2,1)S(1)} %bitcast.245), channel_id=1, replica_groups=mesh['dp'=8,'fsdp'=4] {'fsdp'}, dimensions={0}, use_global_device_ids=true | all-gather | bytes 1244160 | tf_op jit(solution)/shard_map/all_gather | solution.py:57
  55.6 15.8 all-gather.1
  73.3 24.5 %all-gather.18.cloned.1.call-done = bf16[576,1152]{0,1:T(8,128)(2,1)} async-done(((bf16[576,288]{0,1:T(8,128)(2,1)}), bf16[576,1152]{0,1:T(8,128)(2,1)}) %all-gather.18.cloned.1.call-update) | async-done | bytes 1327120 | tf_op jit(solution)/shard_map/all_gather | solution.py:60
  102.9 16.8 all-reduce.16
  119.7 13.1 all-gather.2
  135.2 69.7 %all-reduce.25.cloned.1.call-done = (f32[8,6912]{1,0:T(8,128)}, f32[8,6912]{1,0:T(8,128)}) async-done(((f32[8,6912]{1,0:T(8,128)}, f32[8,6912]{1,0:T(8,128)}), (f32[8,6912]{1,0:T(8,128)}, f32[8,6912]{1,0:T(8,128)})) %all-reduce.25.cloned.1.call-update) | async-done | bytes 442384 | tf_op jit(solution)/shard_map/psum | solution.py:141
  217.8 6.2 fusion
  238.5 12.5 all-gather.16.cloned.1.call-done
  251.0 7.1 convolution_add_fusion.1
  258.2 58.6 %all-gather.20.cloned.1.call-done = bf16[4608,1152]{1,0:T(8,128)(2,1)} async-done(((bf16[576,1152]{1,0:T(8,128)(2,1)}), bf16[4608,1152]{1,0:T(8,128)(2,1)}) %all-gather.20.cloned.1.call-update) | async-done | bytes 10616848 | tf_op jit(solution)/shard_map/all_gather | solution.py:70
  316.8 8.8 fusion.139
  331.1 8.6 fusion.141
  363.6 6.0 fusion.160
  369.7 7.6 fusion.55
  378.1 20.2 %all-reduce.15 = (bf16[1152]{0:T(1024)(128)(2,1)S(1)}, bf16[2304]{0:T(1024)(128)(2,1)}, bf16[2304]{0:T(1024)(128)(2,1)}, bf16[1152]{0:T(1024)(128)(2,1)}, bf16[1...) all-reduce(bf16[1152]{0:T(1024)(128)(2,1)S(1)} %copy-done.101, ...), channel_id=1, replica_groups=mesh['dp'=8,'fsdp'=4] {'fsdp'}, use_global_device_ids=true, to_apply=%add.2 | all-reduce | flops 19584 | bytes 78336
  399.2 6.5 convolution_add_fusion.7
  437.4 5.6 convolution_convert_fusion
  456.2 14.8 copy.162
  477.7 15.3 copy.160
  493.1 315.4 %all-reduce.23.cloned.1.call-done = (f32[8,6912]{1,0:T(8,128)}, f32[8,6912]{1,0:T(8,128)}) async-done(((f32[8,6912]{1,0:T(8,128)}, f32[8,6912]{1,0:T(8,128)}), (f32[8,6912]{1,0:T(8,128)}, f32[8,6912]{1,0:T(8,128)})) %all-reduce.23.cloned.1.call-update) | async-done | bytes 442384 | tf_op jit(solution)/shard_map/psum | solution.py:148
  825.8 168.8 %reduce-scatter.47.cloned.1.call-done = bf16[4608,288]{0,1:T(8,128)(2,1)} async-done(((bf16[4608,1152]{0,1:T(8,128)(2,1)}), bf16[4608,288]{0,1:T(8,128)(2,1)}) %reduce-scatter.47.cloned.1.call-update) | async-done | bytes 2654224 | tf_op jit(solution)/shard_map/reduce_scatter | solution.py:95
  999.5 179.6 %reduce-scatter.45.cloned.1.call-done = bf16[4608,288]{0,1:T(8,128)(2,1)} async-done(((bf16[4608,1152]{0,1:T(8,128)(2,1)}), bf16[4608,288]{0,1:T(8,128)(2,1)}) %reduce-scatter.45.cloned.1.call-update) | async-done | bytes 2654224 | tf_op jit(solution)/shard_map/reduce_scatter | solution.py:95
  1183.8 179.3 %reduce-scatter.59.cloned.1.call-done = bf16[1152,1152]{1,0:T(8,128)(2,1)} async-done(((bf16[4608,1152]{1,0:T(8,128)(2,1)}), bf16[1152,1152]{1,0:T(8,128)(2,1)}) %reduce-scatter.59.cloned.1.call-update) | async-done | bytes 2654224
  1368.5 178.4 %reduce-scatter.57.cloned.1.call-done = bf16[1152,1152]{1,0:T(8,128)(2,1)} async-done(((bf16[4608,1152]{1,0:T(8,128)(2,1)}), bf16[1152,1152]{1,0:T(8,128)(2,1)}) %reduce-scatter.57.cloned.1.call-update) | async-done | bytes 2654224
  1557.3 24.7 %all-reduce.14 = (f32[576]{0:T(1024)}, f32[288]{0:T(512)}, f32[1152]{0:T(1024)}, f32[288]{0:T(512)}) all-reduce(f32[576]{0:T(1024)S(1)} %convert_add_fusion.7, f32[288]{0:T(512)S(1)} %convert_add_fusion.9, f32[1152]{0:T(1024)S(1)} %convert_add_fusion.6, f32[288]{0:T(512)S(1)} %convert_add_fusion.8), channel_id=1, replica_groups=mesh['dp'=8,'fsdp'=4] {'dp'}, use_global_device_ids=true, to_apply=%region_36.37 | all-reduce | flops 2304 | bytes 18432 | tf_op jit(solution)/shard_map/psum | solution.py:125
  1590.9 33.9 %reduce-scatter.53.cloned.1.call-done = bf16[144,288]{1,0:T(8,128)(2,1)} async-done(((bf16[1152,288]{1,0:T(8,128)(2,1)}), bf16[144,288]{1,0:T(8,128)(2,1)}) %reduce-scatter.53.cloned.1.call-update) | async-done | bytes 82960
  1626.6 42.2 %reduce-scatter.51.cloned.1.call-done = bf16[144,864]{1,0:T(8,128)(2,1)} async-done(((bf16[1152,864]{1,0:T(8,128)(2,1)}), bf16[144,864]{1,0:T(8,128)(2,1)}) %reduce-scatter.51.cloned.1.call-update) | async-done | bytes 248848
  1669.9 43.3 %reduce-scatter.49.cloned.1.call-done = bf16[144,864]{1,0:T(8,128)(2,1)} async-done(((bf16[1152,864]{1,0:T(8,128)(2,1)}), bf16[144,864]{1,0:T(8,128)(2,1)}) %reduce-scatter.49.cloned.1.call-update) | async-done | bytes 248848
  1715.6 49.3 %reduce-scatter.63.cloned.1.call-done = bf16[576,288]{1,0:T(8,128)(2,1)} async-done(((bf16[4608,288]{1,0:T(8,128)(2,1)}), bf16[576,288]{1,0:T(8,128)(2,1)}) %reduce-scatter.63.cloned.1.call-update) | async-done | bytes 331792
  1766.1 50.2 %reduce-scatter.61.cloned.1.call-done = bf16[576,288]{1,0:T(8,128)(2,1)} async-done(((bf16[4608,288]{1,0:T(8,128)(2,1)}), bf16[576,288]{1,0:T(8,128)(2,1)}) %reduce-scatter.61.cloned.1.call-update) | async-done | bytes 331792
  1818.5 45.1 %reduce-scatter.43.cloned.1.call-done = bf16[144,1152]{1,0:T(8,128)(2,1)} async-done(((bf16[1152,1152]{1,0:T(8,128)(2,1)}), bf16[144,1152]{1,0:T(8,128)(2,1)}) %reduce-scatter.43.cloned.1.call-update) | async-done | bytes 331792 | tf_op jit(solution)/shard_map/reduce_scatter | solution.py:118
  1863.5 47.7 %reduce-scatter.41.cloned.1.call-done = bf16[144,1152]{1,0:T(8,128)(2,1)} async-done(((bf16[1152,1152]{1,0:T(8,128)(2,1)}), bf16[144,1152]{1,0:T(8,128)(2,1)}) %reduce-scatter.41.cloned.1.call-update) | async-done | bytes 331792 | tf_op jit(solution)/shard_map/reduce_scatter | solution.py:118
  (539 shorter events, 184.6 us)
Async XLA Ops:
  8.0 64.7 %all-gather.14.cloned.1.call-start = ((), (), s32[]{:S(2)}) async-start(), calls=%async_computation.18 | async-start | bytes 1658880 | tf_op jit(solution)/shard_map/all_gather | solution.py:59
  8.8 89.0 %all-gather.18.cloned.1.call-start = ((), (), s32[]{:S(2)}) async-start(), calls=%async_computation.20 | async-start | bytes 1843200 | tf_op jit(solution)/shard_map/all_gather | solution.py:60
  9.5 195.4 %all-reduce.25.cloned.1.call-start = ((), (), s32[]{:S(2)}) async-start(), calls=%async_computation.40 | async-start | bytes 884736 | tf_op jit(solution)/shard_map/psum | solution.py:141
  14.6 195.0 %all-gather.10.cloned.1.call-start = ((), (), s32[]{:S(2)}) async-start(), calls=%async_computation.16 | async-start | bytes 8957952 | tf_op jit(solution)/shard_map/all_gather | solution.py:67
  55.6 172.4 %all-gather.12.cloned.1.call-start = ((), (), s32[]{:S(2)}) async-start(), calls=%async_computation.17 | async-start | bytes 2985984 | tf_op jit(solution)/shard_map/all_gather | solution.py:68
  72.6 178.4 %all-gather.16.cloned.1.call-start = ((), (), s32[]{:S(2)}) async-start(), calls=%async_computation.19 | async-start | bytes 11943936 | tf_op jit(solution)/shard_map/all_gather | solution.py:69
  73.3 60.7 %copy-start.17 = (bf16[2,64,1152]{2,1,0:T(8,128)(2,1)S(1)}, bf16[2,64,1152]{2,1,0:T(8,128)(2,1)}, u32[]{:S(2)}) copy-start(bf16[2,64,1152]{2,1,0:T(8,128)(2,1)} %param.15) | copy-start | bytes 884740
  73.3 243.5 %all-gather.20.cloned.1.call-start = ((), (), s32[]{:S(2)}) async-start(), calls=%async_computation.21 | async-start | bytes 11943936 | tf_op jit(solution)/shard_map/all_gather | solution.py:70
  100.4 708.0 %all-reduce.23.cloned.1.call-start = ((), (), s32[]{:S(2)}) async-start(), calls=%async_computation.39 | async-start | bytes 884736 | tf_op jit(solution)/shard_map/psum | solution.py:148
  134.1 75.1 %copy-start.106 = (f32[64]{0:T(128)}, f32[64]{0:T(128)S(1)}, u32[]{:S(2)}) copy-start(f32[64]{0:T(128)S(1)} %broadcast_multiply_fusion.3) | copy-start | bytes 772
  134.1 75.1 %copy-start.109 = (f32[64]{0:T(128)}, f32[64]{0:T(128)S(1)}, u32[]{:S(2)}) copy-start(f32[64]{0:T(128)S(1)} %broadcast_multiply_fusion.1) | copy-start | bytes 772
  134.9 74.3 %copy-start.129 = (f32[64]{0:T(128)}, f32[64]{0:T(128)S(1)}, u32[]{:S(2)}) copy-start(f32[64]{0:T(128)S(1)} %fusion.129) | copy-start | bytes 772
  135.0 74.3 %copy-start.131 = (f32[64]{0:T(128)}, f32[64]{0:T(128)S(1)}, u32[]{:S(2)}) copy-start(f32[64]{0:T(128)S(1)} %fusion.131) | copy-start | bytes 772
  135.0 72.7 %copy-start.118 = (s32[64]{0:T(128)}, s32[64]{0:T(128)S(1)}, u32[]{:S(2)}) copy-start(s32[64]{0:T(128)S(1)} %get-tuple-element.151) | copy-start | bytes 772
  135.0 72.7 %copy-start.120 = (s32[64]{0:T(128)}, s32[64]{0:T(128)S(1)}, u32[]{:S(2)}) copy-start(s32[64]{0:T(128)S(1)} %get-tuple-element.152) | copy-start | bytes 772
  417.3 395.2 %reduce-scatter.39.cloned.1.call-start = ((), (), s32[]{:S(2)}) async-start(), calls=%async_computation.25 | async-start | bytes 3317760 | tf_op jit(solution)/shard_map/reduce_scatter | solution.py:89
  420.1 394.8 %reduce-scatter.37.cloned.1.call-start = ((), (), s32[]{:S(2)}) async-start(), calls=%async_computation.24 | async-start | bytes 3317760 | tf_op jit(solution)/shard_map/reduce_scatter | solution.py:89
  423.5 393.9 %reduce-scatter.35.cloned.1.call-start = ((), (), s32[]{:S(2)}) async-start(), calls=%async_computation.23 | async-start | bytes 9953280 | tf_op jit(solution)/shard_map/reduce_scatter | solution.py:86
  430.1 391.6 %reduce-scatter.33.cloned.1.call-start = ((), (), s32[]{:S(2)}) async-start(), calls=%async_computation.22 | async-start | bytes 9953280 | tf_op jit(solution)/shard_map/reduce_scatter | solution.py:86
  436.5 558.1 %reduce-scatter.47.cloned.1.call-start = ((), (), s32[]{:S(2)}) async-start(), calls=%async_computation.29 | async-start | bytes 13271040 | tf_op jit(solution)/shard_map/reduce_scatter | solution.py:95
  443.1 735.9 %reduce-scatter.45.cloned.1.call-start = ((), (), s32[]{:S(2)}) async-start(), calls=%async_computation.28 | async-start | bytes 13271040 | tf_op jit(solution)/shard_map/reduce_scatter | solution.py:95
  449.6 913.6 %reduce-scatter.59.cloned.1.call-start = ((), (), s32[]{:S(2)}) async-start(), calls=%async_computation.35 | async-start | bytes 13271040
  471.0 1075.9 %reduce-scatter.57.cloned.1.call-start = ((), (), s32[]{:S(2)}) async-start(), calls=%async_computation.34 | async-start | bytes 13271040
  493.0 1094.6 %all-reduce.21.cloned.1.call-start = ((), (), s32[]{:S(2)}) async-start(), calls=%async_computation.38 | async-start | bytes 147456 | tf_op jit(solution)/shard_map/psum | solution.py:157
  812.5 777.4 %reduce-scatter.55.cloned.1.call-start = ((), (), s32[]{:S(2)}) async-start(), calls=%async_computation.33 | async-start | bytes 995328
  814.9 809.8 %reduce-scatter.53.cloned.1.call-start = ((), (), s32[]{:S(2)}) async-start(), calls=%async_computation.32 | async-start | bytes 995328
  817.4 851.4 %reduce-scatter.51.cloned.1.call-start = ((), (), s32[]{:S(2)}) async-start(), calls=%async_computation.31 | async-start | bytes 2322432
  821.6 891.6 %reduce-scatter.49.cloned.1.call-start = ((), (), s32[]{:S(2)}) async-start(), calls=%async_computation.30 | async-start | bytes 2322432
  825.8 939.0 %reduce-scatter.63.cloned.1.call-start = ((), (), s32[]{:S(2)}) async-start(), calls=%async_computation.37 | async-start | bytes 3981312
  999.4 816.9 %reduce-scatter.61.cloned.1.call-start = ((), (), s32[]{:S(2)}) async-start(), calls=%async_computation.36 | async-start | bytes 3981312
  1183.8 679.8 %reduce-scatter.43.cloned.1.call-start = ((), (), s32[]{:S(2)}) async-start(), calls=%async_computation.27 | async-start | bytes 2985984 | tf_op jit(solution)/shard_map/reduce_scatter | solution.py:118
  1368.4 542.8 %reduce-scatter.41.cloned.1.call-start = ((), (), s32[]{:S(2)}) async-start(), calls=%async_computation.26 | async-start | bytes 2985984 | tf_op jit(solution)/shard_map/reduce_scatter | solution.py:118
  (141 other events, 917.9 us)
Sparse Core Ops, SparseCore 0:
  10.5 50.6 all-gather.13
  62.9 34.8 all-gather.17
  100.4 51.8 all-gather.9
  154.8 30.4 all-gather.11
  187.2 63.8 all-gather.15
  252.9 63.8 all-gather.19
  420.4 50.7 reduce-scatter.38
  473.6 52.8 reduce-scatter.36
  528.8 138.6 reduce-scatter.34
  669.8 140.9 reduce-scatter.32
  813.2 181.4 reduce-scatter.46
  997.0 181.9 reduce-scatter.44
  1181.4 181.7 reduce-scatter.58
  1365.5 181.3 reduce-scatter.56
  1550.0 36.2 reduce-scatter.54
  1589.7 35.0 reduce-scatter.52
  1627.9 40.8 reduce-scatter.50
  1672.4 40.8 reduce-scatter.48
  1716.7 48.0 reduce-scatter.62
  1768.2 48.0 reduce-scatter.60
  1819.8 43.7 reduce-scatter.42
  1867.4 43.7 reduce-scatter.40
Sparse Core Ops, SparseCore 1:
  16.0 188.9 all-reduce.24
  417.4 391.0 all-reduce.22
  814.5 555.3 all-reduce.20
where the time goes:
time: 1930 us; the launch traced here: 1920 us
  waiting for transfers between devices  1500 us (78%)
  matrix products  134 us (7%)
  blocking collectives  129 us (7%)
  local copies, waits for them, and re-layouts  106 us (5%)
  other arithmetic  27.3 us (1%)
  between operations  21.9 us (1%)
    unnamed x33, waiting for transfers between devices  579 us
    reduce_scatter x2, waiting for transfers between devices, reduce_grads(): lax.psum_scatter(full_w[3].astype(jnp.bfloat16), 'fsdp', scatter_dimensio...  348 us
    psum x1, waiting for transfers between devices, ada_grads_sharded(): d_total = lax.psum(d_modulation, ('dp', 'fsdp'))  315 us
    reduce_scatter x2, waiting for transfers between devices, reduce_grads(): lax.psum_scatter(inner_sums[2].astype(jnp.bfloat16), 'dp', scatter_dimens...  92.7 us
    unnamed x328, local copies, waits for them, and re-layouts  89.1 us
    psum x1, waiting for transfers between devices, modulation_sharded(): return lax.psum(padded, ('dp', 'fsdp'))  69.7 us
    all_gather x1, waiting for transfers between devices, gather_weights(): lax.all_gather(inner_parts[3], 'dp', axis=0, tiled=True)  58.6 us
    dot_general x8, matrix products, matmul_right_t(): lax.dot_general(left, right, (((1,), (1,)), ((), ())), preferred_element_...  41 us
  transfers between devices with their start and end apart: 25, of which 16 were waited for; matrix products, arithmetic and copies ran while one was open for 9% of the time, Pallas kernels for 0%

commit v1 on v0

--- a/solution.py
+++ b/solution.py
@@ -1,3 +1,4 @@
+import functools
 import math
 import jax
 import jax.numpy as jnp
@@ -9,6 +10,13 @@
 GELU_C = math.sqrt(2.0 / math.pi)
 PRECISE = lax.Precision.HIGHEST
 NEG_FILL = -1e30
+
+
+def _pair_packet(v0, mesh_dim, row_axis):
+    return lax.psum(lax.psum(v0, mesh_dim), row_axis)
+
+
+produce_sector = functools.partial(_pair_packet, mesh_dim="fsdp", row_axis="dp")
 
 
 def layer_norm(values):
@@ -138,7 +146,7 @@
     partial_value = partial_value + bias_term[None, :]
     padded = jnp.zeros((silu_low.shape[0], col_width * lax.axis_size("fsdp")), jnp.float32)
     padded = lax.dynamic_update_slice_in_dim(padded, partial_value, col_start, 1)
-    return lax.psum(padded, ("dp", "fsdp"))
+    return produce_sector(padded)
 
 
 def ada_grads_sharded(silu_low, cond_rows, d_modulation, w_ada):

time: 1930 us -> 2270 us (1.18)
  waiting for transfers between devices: 1500 us -> 1850 us
    reduce_scatter x2, waiting for transfers between devices: 0.04 us -> 275 us  [reduce_grads(): lax.psum_scatter(full_w[0].astype(jnp.bfloat16), 'fsdp', scatter_dimensio...]
    psum x1, waiting for transfers between devices: 315 us -> 47.9 us  [ada_grads_sharded(): d_total = lax.psum(d_modulation, ('dp', 'fsdp'))]
    reduce_scatter x2, waiting for transfers between devices: 0.04 us -> 104 us  [reduce_grads(): lax.psum_scatter(full_w[1].astype(jnp.bfloat16), 'fsdp', scatter_dimensio...]
    psum x1, waiting for transfers between devices: 0.01 us -> 84.6 us  [ada_grads_sharded(): d_silu = lax.psum(padded, ('dp', 'fsdp'))]
    all_gather x1, waiting for transfers between devices: 0.02 us -> 49.9 us  [gather_weights(): lax.all_gather(inner_parts[0], 'dp', axis=0, tiled=True)]
    all_gather x1, waiting for transfers between devices: 12.5 us -> 55.8 us  [gather_weights(): lax.all_gather(inner_parts[2], 'dp', axis=0, tiled=True)]
    unnamed x33 -> x34, waiting for transfers between devices: 579 us -> 620 us
    psum x1 -> x2, waiting for transfers between devices: 69.7 us -> 58.6 us  [_pair_packet(): return lax.psum(lax.psum(v0, mesh_dim), row_axis)]
  transfers between devices with their start and end apart: 25 -> 26, of which waited for: 16 -> 25; matrix products, arithmetic and copies ran while one was open for 9% -> 8% of each run, Pallas kernels for 0% -> 0%
where the time goes in v1:
time: 2270 us; the launch traced here: 2260 us
  waiting for transfers between devices  1850 us (81%)
  matrix products  131 us (6%)
  blocking collectives  124 us (5%)
  local copies, waits for them, and re-layouts  106 us (5%)
  other arithmetic  26.8 us (1%)
    unnamed x34, waiting for transfers between devices  620 us
    reduce_scatter x2, waiting for transfers between devices, reduce_grads(): lax.psum_scatter(full_w[3].astype(jnp.bfloat16), 'fsdp', scatter_dimensio...  358 us
    reduce_scatter x2, waiting for transfers between devices, reduce_grads(): lax.psum_scatter(full_w[0].astype(jnp.bfloat16), 'fsdp', scatter_dimensio...  275 us
    reduce_scatter x2, waiting for transfers between devices, reduce_grads(): lax.psum_scatter(full_w[1].astype(jnp.bfloat16), 'fsdp', scatter_dimensio...  104 us
    reduce_scatter x2, waiting for transfers between devices, reduce_grads(): lax.psum_scatter(inner_sums[2].astype(jnp.bfloat16), 'dp', scatter_dimens...  92.6 us
    unnamed x302, local copies, waits for them, and re-layouts  88.2 us
    psum x1, waiting for transfers between devices, ada_grads_sharded(): d_silu = lax.psum(padded, ('dp', 'fsdp'))  84.6 us
    all_gather x1, waiting for transfers between devices, gather_weights(): lax.all_gather(inner_parts[3], 'dp', axis=0, tiled=True)  58.7 us
  transfers between devices with their start and end apart: 26, of which 25 were waited for; matrix products, arithmetic and copies ran while one was open for 8% of the time, Pallas kernels for 0%

profile of v1, /device:TPU:0, one launch (start us, length us, event | category | flops | bytes accessed | tf_op | source)
XLA Modules:
  0.0 2260.6 jit_solution(2335090400972777260)
XLA Ops:
  13.6 38.5 %all-reduce.29.cloned.1.call-done = (f32[8,6912]{1,0:T(8,128)}, f32[8,6912]{1,0:T(8,128)}) async-done(((f32[8,6912]{1,0:T(8,128)}, f32[8,6912]{1,0:T(8,128)}), (f32[8,6912]{1,0:T(8,128)}, f32[8,6912]{1,0:T(8,128)})) %all-reduce.29.cloned.1.call-update) | async-done | bytes 442384 | tf_op jit(solution)/shard_map/psum | solution.py:16
  52.2 29.3 %all-gather = bf16[4,864,144]{1,2,0:T(8,128)(2,1)S(1)} all-gather(bf16[1,864,144]{1,2,0:T(8,128)(2,1)S(1)} %bitcast.245), channel_id=1, replica_groups=mesh['dp'=8,'fsdp'=4] {'fsdp'}, dimensions={0}, use_global_device_ids=true | all-gather | bytes 1244160 | tf_op jit(solution)/shard_map/all_gather | solution.py:65
  83.7 19.8 all-gather.1
  105.6 31.0 %all-gather.18.cloned.1.call-done = bf16[576,1152]{0,1:T(8,128)(2,1)} async-done(((bf16[576,288]{0,1:T(8,128)(2,1)}), bf16[576,1152]{0,1:T(8,128)(2,1)}) %all-gather.18.cloned.1.call-update) | async-done | bytes 1327120 | tf_op jit(solution)/shard_map/all_gather | solution.py:68
  141.7 16.6 all-reduce.17
  173.3 20.0 all-reduce.27.cloned.1.call-done
  197.8 49.9 %all-gather.10.cloned.1.call-done = bf16[1152,3456]{1,0:T(8,128)(2,1)} async-done(((bf16[144,3456]{1,0:T(8,128)(2,1)}), bf16[1152,3456]{1,0:T(8,128)(2,1)}) %all-gather.10.cloned.1.call-update) | async-done | bytes 7962640 | tf_op jit(solution)/shard_map/all_gather | solution.py:75
  264.8 15.7 all-gather.12.cloned.1.call-done
  290.6 55.8 %all-gather.16.cloned.1.call-done = bf16[1152,4608]{1,0:T(8,128)(2,1)} async-done(((bf16[144,4608]{1,0:T(8,128)(2,1)}), bf16[1152,4608]{1,0:T(8,128)(2,1)}) %all-gather.16.cloned.1.call-update) | async-done | bytes 10616848 | tf_op jit(solution)/shard_map/all_gather | solution.py:77
  353.5 58.7 %all-gather.20.cloned.1.call-done = bf16[4608,1152]{1,0:T(8,128)(2,1)} async-done(((bf16[576,1152]{1,0:T(8,128)(2,1)}), bf16[4608,1152]{1,0:T(8,128)(2,1)}) %all-gather.20.cloned.1.call-update) | async-done | bytes 10616848 | tf_op jit(solution)/shard_map/all_gather | solution.py:78
  472.4 20.2 all-reduce.16
  550.2 15.2 copy.162
  572.0 15.3 copy.160
  587.4 47.9 %all-reduce.25.cloned.1.call-done = (f32[8,6912]{1,0:T(8,128)}, f32[8,6912]{1,0:T(8,128)}) async-done(((f32[8,6912]{1,0:T(8,128)}, f32[8,6912]{1,0:T(8,128)}), (f32[8,6912]{1,0:T(8,128)}, f32[8,6912]{1,0:T(8,128)})) %all-reduce.25.cloned.1.call-update) | async-done | bytes 442384 | tf_op jit(solution)/shard_map/psum | solution.py:156
  639.4 51.7 %reduce-scatter.39.cloned.1.call-done = bf16[1152,288]{0,1:T(8,128)(2,1)} async-done(((bf16[1152,1152]{0,1:T(8,128)(2,1)}), bf16[1152,288]{0,1:T(8,128)(2,1)}) %reduce-scatter.39.cloned.1.call-update) | async-done | bytes 663568 | tf_op jit(solution)/shard_map/reduce_scatter | solution.py:97
  693.5 52.3 %reduce-scatter.37.cloned.1.call-done = bf16[1152,288]{0,1:T(8,128)(2,1)} async-done(((bf16[1152,1152]{0,1:T(8,128)(2,1)}), bf16[1152,288]{0,1:T(8,128)(2,1)}) %reduce-scatter.37.cloned.1.call-update) | async-done | bytes 663568 | tf_op jit(solution)/shard_map/reduce_scatter | solution.py:97
  748.2 137.6 %reduce-scatter.35.cloned.1.call-done = bf16[1152,864]{0,1:T(8,128)(2,1)} async-done(((bf16[1152,3456]{0,1:T(8,128)(2,1)}), bf16[1152,864]{0,1:T(8,128)(2,1)}) %reduce-scatter.35.cloned.1.call-update) | async-done | bytes 1990672 | tf_op jit(solution)/shard_map/reduce_scatter | solution.py:94
  890.0 137.0 %reduce-scatter.33.cloned.1.call-done = bf16[1152,864]{0,1:T(8,128)(2,1)} async-done(((bf16[1152,3456]{0,1:T(8,128)(2,1)}), bf16[1152,864]{0,1:T(8,128)(2,1)}) %reduce-scatter.33.cloned.1.call-update) | async-done | bytes 1990672 | tf_op jit(solution)/shard_map/reduce_scatter | solution.py:94
  1031.1 178.8 %reduce-scatter.47.cloned.1.call-done = bf16[4608,288]{0,1:T(8,128)(2,1)} async-done(((bf16[4608,1152]{0,1:T(8,128)(2,1)}), bf16[4608,288]{0,1:T(8,128)(2,1)}) %reduce-scatter.47.cloned.1.call-update) | async-done | bytes 2654224 | tf_op jit(solution)/shard_map/reduce_scatter | solution.py:103
  1214.7 178.7 %reduce-scatter.45.cloned.1.call-done = bf16[4608,288]{0,1:T(8,128)(2,1)} async-done(((bf16[4608,1152]{0,1:T(8,128)(2,1)}), bf16[4608,288]{0,1:T(8,128)(2,1)}) %reduce-scatter.45.cloned.1.call-update) | async-done | bytes 2654224 | tf_op jit(solution)/shard_map/reduce_scatter | solution.py:103
  1398.2 178.6 %reduce-scatter.59.cloned.1.call-done = bf16[1152,1152]{1,0:T(8,128)(2,1)} async-done(((bf16[4608,1152]{1,0:T(8,128)(2,1)}), bf16[1152,1152]{1,0:T(8,128)(2,1)}) %reduce-scatter.59.cloned.1.call-update) | async-done | bytes 2654224
  1582.2 178.2 %reduce-scatter.57.cloned.1.call-done = bf16[1152,1152]{1,0:T(8,128)(2,1)} async-done(((bf16[4608,1152]{1,0:T(8,128)(2,1)}), bf16[1152,1152]{1,0:T(8,128)(2,1)}) %reduce-scatter.57.cloned.1.call-update) | async-done | bytes 2654224
  1770.8 24.6 %all-reduce.13 = (f32[576]{0:T(1024)}, f32[288]{0:T(512)}, f32[1152]{0:T(1024)}, f32[288]{0:T(512)}) all-reduce(f32[576]{0:T(1024)S(1)} %convert_add_fusion.7, f32[288]{0:T(512)S(1)} %convert_add_fusion.9, f32[1152]{0:T(1024)S(1)} %convert_add_fusion.6, f32[288]{0:T(512)S(1)} %convert_add_fusion.8), channel_id=1, replica_groups=mesh['dp'=8,'fsdp'=4] {'dp'}, use_global_device_ids=true, to_apply=%region_38.39 | all-reduce | flops 2304 | bytes 18432 | tf_op jit(solution)/shard_map/psum | solution.py:133
  1801.6 84.6 %all-reduce.23.cloned.1.call-done = (f32[8,1152]{1,0:T(8,128)}, f32[8,1152]{1,0:T(8,128)}) async-done(((f32[8,1152]{1,0:T(8,128)}, f32[8,1152]{1,0:T(8,128)}), (f32[8,1152]{1,0:T(8,128)}, f32[8,1152]{1,0:T(8,128)})) %all-reduce.23.cloned.1.call-update) | async-done | bytes 73744 | tf_op jit(solution)/shard_map/psum | solution.py:165
  1888.5 38.2 %reduce-scatter.55.cloned.1.call-done = bf16[144,288]{1,0:T(8,128)(2,1)} async-done(((bf16[1152,288]{1,0:T(8,128)(2,1)}), bf16[144,288]{1,0:T(8,128)(2,1)}) %reduce-scatter.55.cloned.1.call-update) | async-done | bytes 82960
  1927.7 37.5 %reduce-scatter.53.cloned.1.call-done = bf16[144,288]{1,0:T(8,128)(2,1)} async-done(((bf16[1152,288]{1,0:T(8,128)(2,1)}), bf16[144,288]{1,0:T(8,128)(2,1)}) %reduce-scatter.53.cloned.1.call-update) | async-done | bytes 82960
  1967.1 42.3 %reduce-scatter.51.cloned.1.call-done = bf16[144,864]{1,0:T(8,128)(2,1)} async-done(((bf16[1152,864]{1,0:T(8,128)(2,1)}), bf16[144,864]{1,0:T(8,128)(2,1)}) %reduce-scatter.51.cloned.1.call-update) | async-done | bytes 248848
  2010.6 43.5 %reduce-scatter.49.cloned.1.call-done = bf16[144,864]{1,0:T(8,128)(2,1)} async-done(((bf16[1152,864]{1,0:T(8,128)(2,1)}), bf16[144,864]{1,0:T(8,128)(2,1)}) %reduce-scatter.49.cloned.1.call-update) | async-done | bytes 248848
  2056.3 49.3 %reduce-scatter.63.cloned.1.call-done = bf16[576,288]{1,0:T(8,128)(2,1)} async-done(((bf16[4608,288]{1,0:T(8,128)(2,1)}), bf16[576,288]{1,0:T(8,128)(2,1)}) %reduce-scatter.63.cloned.1.call-update) | async-done | bytes 331792
  2106.9 50.2 %reduce-scatter.61.cloned.1.call-done = bf16[576,288]{1,0:T(8,128)(2,1)} async-done(((bf16[4608,288]{1,0:T(8,128)(2,1)}), bf16[576,288]{1,0:T(8,128)(2,1)}) %reduce-scatter.61.cloned.1.call-update) | async-done | bytes 331792
  2159.3 45.1 %reduce-scatter.43.cloned.1.call-done = bf16[144,1152]{1,0:T(8,128)(2,1)} async-done(((bf16[1152,1152]{1,0:T(8,128)(2,1)}), bf16[144,1152]{1,0:T(8,128)(2,1)}) %reduce-scatter.43.cloned.1.call-update) | async-done | bytes 331792 | tf_op jit(solution)/shard_map/reduce_scatter | solution.py:126
  2204.3 47.5 %reduce-scatter.41.cloned.1.call-done = bf16[144,1152]{1,0:T(8,128)(2,1)} async-done(((bf16[1152,1152]{1,0:T(8,128)(2,1)}), bf16[144,1152]{1,0:T(8,128)(2,1)}) %reduce-scatter.41.cloned.1.call-update) | async-done | bytes 331792 | tf_op jit(solution)/shard_map/reduce_scatter | solution.py:126
  (516 shorter events, 250.8 us)
Async XLA Ops:
  7.2 44.9 %all-reduce.29.cloned.1.call-start = ((), (), s32[]{:S(2)}) async-start(), calls=%async_computation.41 | async-start | bytes 884736 | tf_op jit(solution)/shard_map/psum | solution.py:16
  8.7 43.5 %copy-start.86 = (bf16[144,864]{1,0:T(8,128)(2,1)S(1)}, bf16[144,864]{1,0:T(8,128)(2,1)}, u32[]{:S(2)}) copy-start(bf16[144,864]{1,0:T(8,128)(2,1)} %param.22) | copy-start | bytes 746500
  12.0 92.8 %all-gather.14.cloned.1.call-start = ((), (), s32[]{:S(2)}) async-start(), calls=%async_computation.18 | async-start | bytes 1658880 | tf_op jit(solution)/shard_map/all_gather | solution.py:67
  12.8 123.8 %all-gather.18.cloned.1.call-start = ((), (), s32[]{:S(2)}) async-start(), calls=%async_computation.20 | async-start | bytes 1843200 | tf_op jit(solution)/shard_map/all_gather | solution.py:68
  13.5 179.8 %all-reduce.27.cloned.1.call-start = ((), (), s32[]{:S(2)}) async-start(), calls=%async_computation.40 | async-start | bytes 884736 | tf_op jit(solution)/shard_map/psum | solution.py:16
  52.1 195.6 %all-gather.10.cloned.1.call-start = ((), (), s32[]{:S(2)}) async-start(), calls=%async_computation.16 | async-start | bytes 8957952 | tf_op jit(solution)/shard_map/all_gather | solution.py:75
  83.7 196.8 %all-gather.12.cloned.1.call-start = ((), (), s32[]{:S(2)}) async-start(), calls=%async_computation.17 | async-start | bytes 2985984 | tf_op jit(solution)/shard_map/all_gather | solution.py:76
  104.8 241.6 %all-gather.16.cloned.1.call-start = ((), (), s32[]{:S(2)}) async-start(), calls=%async_computation.19 | async-start | bytes 11943936 | tf_op jit(solution)/shard_map/all_gather | solution.py:77
  105.5 52.8 %copy-start.109 = (bf16[1152]{0:T(1024)(128)(2,1)S(1)}, bf16[1152]{0:T(1024)(128)(2,1)}, u32[]{:S(2)}) copy-start(bf16[1152]{0:T(1024)(128)(2,1)} %param.27) | copy-start | bytes 6916
  105.6 66.0 %copy-start.121 = (bf16[288]{0:T(512)(128)(2,1)S(1)}, bf16[288]{0:T(512)(128)(2,1)}, u32[]{:S(2)}) copy-start(bf16[288]{0:T(512)(128)(2,1)} %param.29) | copy-start | bytes 1732
  105.6 66.5 %copy-start.17 = (bf16[2,64,1152]{2,1,0:T(8,128)(2,1)S(1)}, bf16[2,64,1152]{2,1,0:T(8,128)(2,1)}, u32[]{:S(2)}) copy-start(bf16[2,64,1152]{2,1,0:T(8,128)(2,1)} %param.15) | copy-start | bytes 884740
  105.6 306.7 %all-gather.20.cloned.1.call-start = ((), (), s32[]{:S(2)}) async-start(), calls=%async_computation.21 | async-start | bytes 11943936 | tf_op jit(solution)/shard_map/all_gather | solution.py:78
  139.3 496.0 %all-reduce.25.cloned.1.call-start = ((), (), s32[]{:S(2)}) async-start(), calls=%async_computation.39 | async-start | bytes 884736 | tf_op jit(solution)/shard_map/psum | solution.py:156
  197.8 54.6 %copy-start.41 = (bf16[64,1152]{1,0:T(8,128)(2,1)}, bf16[64,1152]{1,0:T(8,128)(2,1)S(1)}, u32[]{:S(2)}) copy-start(bf16[64,1152]{1,0:T(8,128)(2,1)S(1)} %get-tuple-element.142) | copy-start | bytes 442372
  197.8 58.0 %copy-start.39 = (bf16[64,1152]{1,0:T(8,128)(2,1)}, bf16[64,1152]{1,0:T(8,128)(2,1)S(1)}, u32[]{:S(2)}) copy-start(bf16[64,1152]{1,0:T(8,128)(2,1)S(1)} %get-tuple-element.141) | copy-start | bytes 442372
  511.5 179.6 %reduce-scatter.39.cloned.1.call-start = ((), (), s32[]{:S(2)}) async-start(), calls=%async_computation.25 | async-start | bytes 3317760 | tf_op jit(solution)/shard_map/reduce_scatter | solution.py:97
  514.4 231.4 %reduce-scatter.37.cloned.1.call-start = ((), (), s32[]{:S(2)}) async-start(), calls=%async_computation.24 | async-start | bytes 3317760 | tf_op jit(solution)/shard_map/reduce_scatter | solution.py:97
  517.7 368.1 %reduce-scatter.35.cloned.1.call-start = ((), (), s32[]{:S(2)}) async-start(), calls=%async_computation.23 | async-start | bytes 9953280 | tf_op jit(solution)/shard_map/reduce_scatter | solution.py:94
  524.2 502.8 %reduce-scatter.33.cloned.1.call-start = ((), (), s32[]{:S(2)}) async-start(), calls=%async_computation.22 | async-start | bytes 9953280 | tf_op jit(solution)/shard_map/reduce_scatter | solution.py:94
  530.6 679.4 %reduce-scatter.47.cloned.1.call-start = ((), (), s32[]{:S(2)}) async-start(), calls=%async_computation.29 | async-start | bytes 13271040 | tf_op jit(solution)/shard_map/reduce_scatter | solution.py:103
  537.1 856.4 %reduce-scatter.45.cloned.1.call-start = ((), (), s32[]{:S(2)}) async-start(), calls=%async_computation.28 | async-start | bytes 13271040 | tf_op jit(solution)/shard_map/reduce_scatter | solution.py:103
  543.6 1033.2 %reduce-scatter.59.cloned.1.call-start = ((), (), s32[]{:S(2)}) async-start(), calls=%async_computation.35 | async-start | bytes 13271040
  565.4 1195.0 %reduce-scatter.57.cloned.1.call-start = ((), (), s32[]{:S(2)}) async-start(), calls=%async_computation.34 | async-start | bytes 13271040
  587.3 1298.9 %all-reduce.23.cloned.1.call-start = ((), (), s32[]{:S(2)}) async-start(), calls=%async_computation.38 | async-start | bytes 147456 | tf_op jit(solution)/shard_map/psum | solution.py:165
  639.3 1287.4 %reduce-scatter.55.cloned.1.call-start = ((), (), s32[]{:S(2)}) async-start(), calls=%async_computation.33 | async-start | bytes 995328
  693.4 1271.8 %reduce-scatter.53.cloned.1.call-start = ((), (), s32[]{:S(2)}) async-start(), calls=%async_computation.32 | async-start | bytes 995328
  748.1 1261.3 %reduce-scatter.51.cloned.1.call-start = ((), (), s32[]{:S(2)}) async-start(), calls=%async_computation.31 | async-start | bytes 2322432
  889.9 1164.1 %reduce-scatter.49.cloned.1.call-start = ((), (), s32[]{:S(2)}) async-start(), calls=%async_computation.30 | async-start | bytes 2322432
  1031.1 1074.5 %reduce-scatter.63.cloned.1.call-start = ((), (), s32[]{:S(2)}) async-start(), calls=%async_computation.37 | async-start | bytes 3981312
  1214.7 942.4 %reduce-scatter.61.cloned.1.call-start = ((), (), s32[]{:S(2)}) async-start(), calls=%async_computation.36 | async-start | bytes 3981312
  1398.2 806.2 %reduce-scatter.43.cloned.1.call-start = ((), (), s32[]{:S(2)}) async-start(), calls=%async_computation.27 | async-start | bytes 2985984 | tf_op jit(solution)/shard_map/reduce_scatter | solution.py:126
  1582.1 669.8 %reduce-scatter.41.cloned.1.call-start = ((), (), s32[]{:S(2)}) async-start(), calls=%async_computation.26 | async-start | bytes 2985984 | tf_op jit(solution)/shard_map/reduce_scatter | solution.py:126
  (129 other events, 893.2 us)
Sparse Core Ops, SparseCore 0:
  12.2 39.9 all-reduce.28
  53.8 45.6 all-gather.13
  101.1 35.4 all-gather.17
  140.0 53.3 all-reduce.26
  195.8 51.8 all-gather.9
  250.2 30.2 all-gather.11
  282.5 63.8 all-gather.15
  348.4 63.8 all-gather.19
  511.6 123.6 all-reduce.24
  637.4 53.5 reduce-scatter.38
  693.4 52.3 reduce-scatter.36
  748.0 137.7 reduce-scatter.34
  888.3 138.6 reduce-scatter.32
  1029.2 180.6 reduce-scatter.46
  1212.3 181.1 reduce-scatter.44
  1395.7 181.1 reduce-scatter.58
  1579.2 181.1 reduce-scatter.56
  1766.5 119.6 all-reduce.22
  1889.5 37.1 reduce-scatter.54
  1930.1 35.0 reduce-scatter.52
  1968.6 40.7 reduce-scatter.50
  2013.2 40.8 reduce-scatter.48
  2057.5 48.0 reduce-scatter.62
  2109.0 48.0 reduce-scatter.60
  2160.6 43.7 reduce-scatter.42
  2208.1 43.7 reduce-scatter.40
